TPU v7x, 32 devices: a whole 2x2x4 slice. The times are simulated.
32 devices in a mesh: tm: 16 (over z, x, core), chan: 2 (over y).
Axes of the slice: x: 2, y: 2, z: 4, core: 2. Of those that a mesh axis runs over, the one named last changes fastest.
Arguments:
- series: float32 [64, 8192], P('chan', 'tm'), may hold values from -200 to 200
- tail: float32 [64, 127], P('chan'), may hold values from -200 to 200
- excl: int32 [1], replicated, may hold values from 32 to 128
Outputs:
- profile: float32 [8192], P('tm')
All inputs are finite; a program needn't handle non-finite values.
Results may differ from a plain program's by a relative error of at most 0.0003.
Values may be sent and summed in bfloat16 or wider, within the bound.
No kernel may reach another device: no remote copies, remote signals or barrier semaphores. Data moves between devices by JAX's collectives and lax.ppermute only.
A program may use at most 128 MiB of HBM per device.

v0:
```python
import functools
import math

import jax
import jax.numpy as jnp
from jax import lax
from jax.experimental import pallas as pl
from jax.experimental.pallas import tpu as pltpu
from jax.sharding import PartitionSpec as P


EPSILON = 1e-05
CEILING = 4.0
FLOOR = 1.0 - CEILING
LANES = 128
WIDTH = 16


def transposed(value, target):
    length = value.shape[1]
    half = LANES // 2
    ahead = pltpu.roll(value, length - half, 1)
    for start in range(0, length, LANES):
        stop = start + LANES
        both = jnp.concatenate([value[:, start:stop], ahead[:, start:stop]], axis=0)
        target[start:stop, :] = both.T


def statistics(value, sums, moments, mean, scale):
    channels = value.shape[0]
    count = mean.shape[0]
    half = count // 2
    window = value.shape[1] - count
    for start in range(0, half + window, LANES):
        stop = start + LANES
        both = jnp.concatenate([value[:, start:stop], value[:, half + start : half + stop]], axis=0)
        sums[0][start:stop, :] = both.T
    size = 1
    level = 0
    while size < window:
        rows = -(-(half + window - 2 * size) // 8) * 8
        old, new = sums[level % 2], sums[(level + 1) % 2]
        for start in range(0, rows, 64):
            stop = min(start + 64, rows)
            here = old[start:stop, :]
            there = old[start + size : stop + size, :]
            gap = here - there
            square = gap * gap
            if size > 1:
                past = moments[level % 2]
                square += 2.0 * (past[start:stop, :] + past[start + size : stop + size, :])
            new[start:stop, :] = here + there
            moments[(level + 1) % 2][start:stop, :] = square
        level += 1
        size *= 2
    lower = lax.broadcasted_iota(jnp.int32, (64, LANES), 1) < LANES // 2
    for start in range(0, half, 64):
        rows = slice(start, start + 64)
        center = sums[level % 2][rows, :] * (1.0 / window)
        spread = moments[level % 2][rows, :] * (1.0 / (window * window))
        factor = lax.rsqrt(spread + EPSILON) * (1.0 / math.sqrt(window * channels))
        for target, part in ((mean, center), (scale, factor)):
            other = pltpu.roll(part, LANES // 2, 1)
            target[rows, :] = jnp.where(lower, part, other)
            target[half + start : half + start + 64, :] = jnp.where(lower, other, part)


def contract(left, right):
    return lax.dot_general(
        left, right, (((1,), (1,)), ((), ())), preferred_element_type=jnp.float32
    )


def fill(samples, means, scales, zed, step, base):
    for start in range(0, means.shape[0], 16):
        mean = means[start : start + 16, :]
        scale = scales[start : start + 16, :]
        for inner in range(0, WIDTH, 2):
            parts = [
                (samples[pl.ds(step + (start + inner + side), 16), :] - mean) * scale
                for side in range(2)
            ]
            zed[start : start + 16, pl.ds(base + inner * LANES, 2 * LANES)] = (
                jnp.concatenate(parts, axis=1).astype(jnp.bfloat16)
            )


def block_of(index):
    return pl.multiple_of(index * (WIDTH * LANES), WIDTH * LANES)


def gap_of(shape, row_start, column_start):
    rows = lax.broadcasted_iota(jnp.int32, shape, 0) + row_start
    columns = lax.broadcasted_iota(jnp.int32, shape, 1) + column_start
    return rows - columns


def rows_best(value):
    best = value[:, :LANES]
    for start in range(LANES, value.shape[1], LANES):
        best = jnp.maximum(best, value[:, start : start + LANES])
    return jnp.max(best.T, axis=0, keepdims=True)


def own_body(
    info, near, head, tail, zed_out,
    samples, means, scales, sums_a, sums_b, moments_a, moments_b,
):
    last = jnp.where(info[4] > 0, tail[...], head[...])
    value = jnp.concatenate([near[...], last], axis=1)
    transposed(value, samples)
    statistics(value, (sums_a, sums_b), (moments_a, moments_b), means, scales)

    def build(index, carry):
        fill(samples, means, scales, zed_out, index * WIDTH, block_of(index))
        return carry

    lax.fori_loop(0, zed_out.shape[1] // (WIDTH * LANES), build, 0)


def staged(mine, stage, base, chan):
    quarter = mine.shape[0] // 4
    for place in range(2):
        start = pl.multiple_of((2 * place + chan) * quarter, quarter)
        stage[place * quarter : (place + 1) * quarter, :] = mine[
            pl.ds(start, quarter), pl.ds(base, WIDTH * LANES)
        ]


def cross_body(
    info, mine, other, head, tail, away_out, part_out, pair_out,
    samples, means, scales, sums_a, sums_b, moments_a, moments_b, zed_a, zed_b, cross,
    stage_a, stage_b,
):
    count = means.shape[0]
    quarter = count // 4
    limit, shift, valid = info[0], info[2], info[3]
    last = jnp.where(info[5] > 0, tail[...], head[...])
    value = jnp.concatenate([other[...], last], axis=1)
    transposed(value, samples)
    staged(mine, stage_a, block_of(0), info[1])
    product = contract(mine[:, pl.ds(block_of(0), WIDTH * LANES)], stage_a[...])
    pair_out[...] = product
    statistics(value, (sums_a, sums_b), (moments_a, moments_b), means, scales)
    staged(mine, stage_b, block_of(1), info[1])
    product = contract(mine[:, pl.ds(block_of(1), WIDTH * LANES)], stage_b[...])
    pair_out[...] = pair_out[...] + product
    zeds = (zed_a, zed_b)
    cross[...] = jnp.zeros_like(cross)
    fill(samples, means, scales, zed_a, 0, 0)

    def pair(index, carry):
        for slot in range(2):
            block = 2 * index + slot
            cross[...] += contract(
                zeds[slot][...], mine[:, pl.ds(block_of(block), WIDTH * LANES)]
            )
            fill(samples, means, scales, zeds[1 - slot], (block + 1) * WIDTH, 0)
        return carry

    lax.fori_loop(0, mine.shape[1] // (2 * WIDTH * LANES), pair, 0, unroll=True)
    far = jnp.where(
        (gap_of(cross.shape, shift * count, 0) >= limit) & (valid > 0), cross[...], FLOOR
    )
    columns = jnp.max(far, axis=0, keepdims=True)
    for index in range(4):
        rows = slice(index * quarter, (index + 1) * quarter)
        away_out[index : index + 1, :] = 1.0 - rows_best(far[rows, :])
        part_out[index : index + 1, :] = columns[:, rows]


def pair_body(info, mine, part, partial, own_out, stage_a, stage_b, pair):
    count = mine.shape[0]
    quarter = count // 4
    limit, chan = info[0], info[1]
    stages = (stage_a, stage_b)
    starts = [
        pl.multiple_of(chan * quarter, quarter),
        pl.multiple_of(2 * quarter + chan * quarter, quarter),
    ]
    blocks = mine.shape[1] // (WIDTH * LANES)
    for slot in range(2):
        base = block_of(blocks - 2 + slot)
        staged(mine, stages[slot], base, chan)
        value = contract(mine[:, pl.ds(base, WIDTH * LANES)], stages[slot][...])
        pair[...] = (pair if slot else partial)[...] + value
    near = []
    for index, start in enumerate(starts):
        value = pair[:, index * quarter : (index + 1) * quarter]
        near.append(jnp.where(jnp.abs(gap_of(value.shape, 0, start)) >= limit, value, FLOOR))
    lines = [jnp.max(value, axis=0, keepdims=True) for value in near]
    both = jnp.maximum(near[0], near[1])
    for index in range(4):
        best = rows_best(both[index * quarter : (index + 1) * quarter, :])
        best = jnp.maximum(best, part[index : index + 1, :])
        line = jnp.where(chan == index % 2, lines[index // 2], FLOOR)
        own_out[index : index + 1, :] = 1.0 - jnp.maximum(best, line)


SMEM = pl.BlockSpec(memory_space=pltpu.SMEM)
VMEM = pl.BlockSpec(memory_space=pltpu.VMEM)


def sized(*shape, dtype=jnp.float32):
    return jax.ShapeDtypeStruct(shape, dtype)


def working(count, length):
    long, short = pltpu.VMEM((length, LANES), jnp.float32), pltpu.VMEM((count, LANES), jnp.float32)
    return [long, short, short, long, long, long, long]


def settings(flops):
    return dict(
        compiler_params=pltpu.CompilerParams(vmem_limit_bytes=16 << 20),
        cost_estimate=pl.CostEstimate(flops=flops, bytes_accessed=1 << 21, transcendentals=0),
    )


def prepare(info, near, head, tail):
    channels, count = near.shape
    window = head.shape[1]
    return pl.pallas_call(
        own_body,
        out_shape=sized(count, channels * window, dtype=jnp.bfloat16),
        in_specs=[SMEM, VMEM, VMEM, VMEM],
        out_specs=VMEM,
        scratch_shapes=working(count, count + window),
        **settings(count * channels * window * 100),
    )(info, near, head, tail)


def crossed(info, mine, other, head, tail):
    channels, count = other.shape
    window = head.shape[1]
    return pl.pallas_call(
        cross_body,
        out_shape=[sized(4, count // 4)] * 2 + [sized(count, count // 2)],
        in_specs=[SMEM] + [VMEM] * 4,
        out_specs=[VMEM] * 3,
        scratch_shapes=[
            *working(count, count + window),
            *[pltpu.VMEM((count, WIDTH * LANES), jnp.bfloat16)] * 2,
            pltpu.VMEM((count, count), jnp.float32),
            *[pltpu.VMEM((count // 2, WIDTH * LANES), jnp.bfloat16)] * 2,
        ],
        **settings(2 * count * count * channels * window),
    )(info, mine, other, head, tail)


def paired(info, mine, part, partial):
    count, depth = mine.shape
    return pl.pallas_call(
        pair_body,
        out_shape=sized(4, count // 4),
        in_specs=[SMEM] + [VMEM] * 3,
        out_specs=VMEM,
        scratch_shapes=[
            *[pltpu.VMEM((count // 2, WIDTH * LANES), jnp.bfloat16)] * 2,
            pltpu.VMEM((count, count // 2), jnp.float32),
        ],
        **settings(count * count * depth),
    )(info, mine, part, partial)


def on_device(blocks, chans, series, tail, excl):
    return profile(blocks, chans, series, tail, excl)


def profile(blocks, chans, series, tail, excl):
    count = series.shape[1]
    window = tail.shape[1] + 1
    block = lax.axis_index("tm")
    chan = lax.axis_index("chan")
    axes = ("tm", "chan")
    places = [(b, c) for b in range(blocks) for c in range(chans)]

    def shifted(value, reach):
        pairs = [
            ((b + reach(c)) * chans + c, b * chans + c)
            for b, c in places
            if 0 <= b + reach(c) < blocks
        ]
        return lax.ppermute(value, axes, pairs)

    def swapped(value):
        return lax.ppermute(value, "chan", [(c, chans - 1 - c) for c in range(chans)])

    shift = chans - chan
    flags = [block + shift < blocks, block == blocks - 1, block + shift == blocks - 1]
    info = jnp.stack([excl[0], chan, shift] + [flag.astype(jnp.int32) for flag in flags])
    spare = jnp.zeros((series.shape[0], 1), series.dtype)
    partner = swapped(series)
    ends = [(b, c) for b, c in places if b >= blocks - 1 - chans]
    pairs = [(b * chans + c, b * chans + chans - 1 - c) for b, c in ends]
    partner_tail = lax.ppermute(tail, axes, pairs)
    padded = lax.optimization_barrier(jnp.concatenate([series, tail, spare], axis=1))
    near = jnp.concatenate([padded[:, :count], partner], axis=0)
    partner_tail = jnp.concatenate([partner_tail, spare], axis=1)
    ending = jnp.concatenate([padded[:, count:], partner_tail], axis=0)
    other = shifted(near, lambda c: chans - c)
    head = shifted(near[:, :window], lambda c: 1)
    other_head = shifted(near[:, :window], lambda c: chans + 1 - c)
    mine = prepare(info, near, head, ending)
    away, part, partial = crossed(info, mine, other, other_head, ending)
    home = shifted(away, lambda c: c - chans)
    best = paired(info, mine, part, partial)
    best = jnp.minimum(best, jnp.where(block - shift >= 0, home, CEILING))
    return jnp.minimum(best, swapped(best)).reshape(count)


def solution(mesh):
    placed = (P("chan", "tm"), P("chan", None), P())
    run = functools.partial(on_device, mesh.shape["tm"], mesh.shape["chan"])
    return jax.shard_map(run, mesh=mesh, in_specs=placed, out_specs=P("tm"), check_vma=False)
```

profile of v0, /device:TPU:24, one launch (start us, length us, event | category | flops | bytes accessed | tf_op | source)
XLA Modules:
  0.0 34.8 jit_solution(4528003502873809068)
XLA Ops:
  0.0 0.7 %collective-permute-start.2 = (f32[32,127]{1,0:T(8,128)}, f32[32,127]{1,0:T(8,128)S(1)}, u32[]{:S(2)}, u32[]{:S(2)}) collective-permute-start(f32[32,127]{1,0:T(8,128)} %param.4), channel_id=1, source_target_pairs={{26,27},{27,26},{28,29},{29,28},{30,31},{31,30}} | collective-permute-start | bytes 48776 | tf_op jit(solution)/shard_map/ppermute | solution.py:296
  0.7 1.6 %collective-permute-start = (f32[32,512]{1,0:T(8,128)}, f32[32,512]{1,0:T(8,128)S(1)}, u32[]{:S(2)}, u32[]{:S(2)}) collective-permute-start(f32[32,512]{1,0:T(8,128)} %param.3), channel_id=1, source_target_pairs={{0,1},{1,0},{2,3},{3,2},{4,5},{5,4},{6,7},{7,6},{8,9},{9,8},{10,11... | collective-permute-start | bytes 196616 | tf_op jit(solution)/shard_map/ppermute | solution.py:287
  2.2 0.1 pad.7.clone
  2.3 0.9 %maximum_maximum_fusion = f32[32,640]{1,0:T(8,128)S(1)} fusion(f32[32,127]{1,0:T(8,128)} %param.4, f32[32,512]{1,0:T(8,128)} %param.3, f32[640]{0:T(1024)S(1)} %pad.7.clone), kind=kLoop, calls=%fused_computation.3 | loop fusion | flops 40960 | bytes 166272 | tf_op jit(solution)/shard_map/concatenate | solution.py:297
  3.9 0.1 stack.35.info
  4.0 1.4 %collective-permute-done = f32[32,512]{1,0:T(8,128)S(1)} collective-permute-done((f32[32,512]{1,0:T(8,128)}, f32[32,512]{1,0:T(8,128)S(1)}, u32[]{:S(2)}, u32[]{:S(2)}) %collective-permute-start) | collective-permute-done | bytes 65568 | tf_op jit(solution)/shard_map/ppermute | solution.py:287
  5.4 1.9 %collective-permute-start.1 = (f32[64,128]{1,0:T(8,128)S(1)}, f32[64,128]{1,0:T(8,128)S(1)}, u32[]{:S(2)}, u32[]{:S(2)}) collective-permute-start(f32[64,128]{1,0:T(8,128)S(1)} %fusion), channel_id=1, source_target_pairs={{2,0},{3,1},{4,2},{5,3},{6,4},{7,5},{8,6},{9,7},{10,8},{11,9},{12,... | collective-permute-start | bytes 98312 | tf_op jit(solution)/shard_map/ppermute | solution.py:284
  7.3 3.1 %collective-permute-start.3 = (f32[64,512]{1,0:T(8,128)S(1)}, f32[64,512]{1,0:T(8,128)S(1)}, u32[]{:S(2)}, u32[]{:S(2)}) collective-permute-start(f32[64,512]{1,0:T(8,128)S(1)} %pad_maximum_fusion.near), channel_id=1, source_target_pairs={{4,0},{3,1},{6,2},{5,3},{8,4},{7,5},{10,6},{9,7},{12,8},{11,9},{14... | collective-permute-start | bytes 393224 | tf_op jit(solution)/shard_map/ppermute | solution.py:284
  10.4 0.0 collective-permute-done.2
  10.5 2.2 %collective-permute-start.4 = (f32[64,128]{1,0:T(8,128)S(1)}, f32[64,128]{1,0:T(8,128)S(1)}, u32[]{:S(2)}, u32[]{:S(2)}) collective-permute-start(f32[64,128]{1,0:T(8,128)S(1)} %fusion), channel_id=1, source_target_pairs={{6,0},{5,1},{8,2},{7,3},{10,4},{9,5},{12,6},{11,7},{14,8},{13,9},{... | collective-permute-start | bytes 98312 | tf_op jit(solution)/shard_map/ppermute | solution.py:284
  12.6 0.0 collective-permute-done.1.head
  12.7 2.6 %shard_map.37.mine = bf16[512,8192]{1,0:T(8,128)(2,1)S(1)} custom-call(s32[6]{0:T(128)S(1)} %stack.35.info, f32[64,512]{1,0:T(8,128)S(1)} %pad_maximum_fusion.near, f32[64,128]{1,0:T(8,128)S(1)} %collective-permute-done.1.head, f32[64,128]{1,0:T(8,128)S(1)} %select_maximum_fusion.tail), custom_call_target="tpu_custom_call" | custom-call | flops 419430400 | bytes 2097152 | tf_op jit(solution)/shard_map/pallas_call | solution.py:223
  15.3 1.9 %collective-permute-done.4.head = f32[64,128]{1,0:T(8,128)S(1)} collective-permute-done((f32[64,128]{1,0:T(8,128)S(1)}, f32[64,128]{1,0:T(8,128)S(1)}, u32[]{:S(2)}, u32[]{:S(2)}) %collective-permute-start.4) | collective-permute-done | bytes 32800 | tf_op jit(solution)/shard_map/ppermute | solution.py:284
  17.2 0.0 collective-permute-done.3.other
  17.2 7.0 %shard_map.38 = (f32[4,128]{1,0:T(4,128)S(1)}, f32[4,128]{1,0:T(4,128)S(1)}, f32[512,256]{1,0:T(8,128)S(1)}) custom-call(s32[6]{0:T(128)S(1)} %stack.35.info, bf16[512,8192]{1,0:T(8,128)(2,1)S(1)} %shard_map.37.mine, f32[64,512]{1,0:T(8,128)S(1)} %collective-permute-done.3.other, f32[64,128]{1,0:T(8,128)S(1)} %collective-permute-done.4.head, ...), custom_call_target="tpu_custom_call" | custom-call | flops 4294967296 | bytes 2097152 | tf_op jit(solution)/shard_map/pallas_call | solution.py:236
  24.2 1.9 %collective-permute-start.5 = (f32[4,128]{1,0:T(4,128)S(1)}, f32[4,128]{1,0:T(4,128)S(1)}, u32[]{:S(2)}, u32[]{:S(2)}) collective-permute-start(f32[4,128]{1,0:T(4,128)S(1)} %get-tuple-element.10), channel_id=1, source_target_pairs={{1,3},{0,4},{3,5},{2,6},{5,7},{4,8},{7,9},{6,10},{9,11},{8,12},{11... | collective-permute-start | bytes 6152 | tf_op jit(solution)/shard_map/ppermute | solution.py:284
  26.1 1.9 %shard_map.39 = f32[4,128]{1,0:T(4,128)S(1)} custom-call(s32[6]{0:T(128)S(1)} %stack.35.info, bf16[512,8192]{1,0:T(8,128)(2,1)S(1)} %shard_map.37.mine, f32[4,128]{1,0:T(4,128)S(1)} %get-tuple-element.8.part, f32[512,256]{1,0:T(8,128)S(1)} %get-tuple-element.9.partial), custom_call_target="tpu_custom_call" | custom-call | flops 2147483648 | bytes 2097152 | tf_op jit(solution)/shard_map/pallas_call | solution.py:253
  28.1 2.5 %collective-permute-done.5 = f32[4,128]{1,0:T(4,128)S(1)} collective-permute-done((f32[4,128]{1,0:T(4,128)S(1)}, f32[4,128]{1,0:T(4,128)S(1)}, u32[]{:S(2)}, u32[]{:S(2)}) %collective-permute-start.5) | collective-permute-done | bytes 2080 | tf_op jit(solution)/shard_map/ppermute | solution.py:284
  30.6 0.1 collective-permute-start.6
  30.7 3.5 %collective-permute-done.6 = f32[4,128]{1,0:T(4,128)S(1)} collective-permute-done((f32[4,128]{1,0:T(4,128)S(1)}, f32[4,128]{1,0:T(4,128)S(1)}, u32[]{:S(2)}, u32[]{:S(2)}) %collective-permute-start.6) | collective-permute-done | bytes 2080 | tf_op jit(solution)/shard_map/ppermute | solution.py:287
  34.2 0.6 %minimum_bitcast_fusion = f32[512]{0:T(512)} fusion(f32[4,128]{1,0:T(4,128)S(1)} %select_minimum_fusion, f32[4,128]{1,0:T(4,128)S(1)} %collective-permute-done.6), kind=kLoop, calls=%fused_computation.7 | loop fusion | flops 512 | bytes 6144 | tf_op jit(solution)/shard_map/reshape | solution.py:309
  (6 shorter events, 0.0 us)
Async XLA Ops:
  0.0 10.4 %collective-permute-start.2 = (f32[32,127]{1,0:T(8,128)}, f32[32,127]{1,0:T(8,128)S(1)}, u32[]{:S(2)}, u32[]{:S(2)}) collective-permute-start(f32[32,127]{1,0:T(8,128)} %param.4), channel_id=1, source_target_pairs={{26,27},{27,26},{28,29},{29,28},{30,31},{31,30}} | collective-permute-start | bytes 48776 | tf_op jit(solution)/shard_map/ppermute | solution.py:296
  0.7 4.7 %collective-permute-start = (f32[32,512]{1,0:T(8,128)}, f32[32,512]{1,0:T(8,128)S(1)}, u32[]{:S(2)}, u32[]{:S(2)}) collective-permute-start(f32[32,512]{1,0:T(8,128)} %param.3), channel_id=1, source_target_pairs={{0,1},{1,0},{2,3},{3,2},{4,5},{5,4},{6,7},{7,6},{8,9},{9,8},{10,11... | collective-permute-start | bytes 196616 | tf_op jit(solution)/shard_map/ppermute | solution.py:287
  5.4 7.3 %collective-permute-start.1 = (f32[64,128]{1,0:T(8,128)S(1)}, f32[64,128]{1,0:T(8,128)S(1)}, u32[]{:S(2)}, u32[]{:S(2)}) collective-permute-start(f32[64,128]{1,0:T(8,128)S(1)} %fusion), channel_id=1, source_target_pairs={{2,0},{3,1},{4,2},{5,3},{6,4},{7,5},{8,6},{9,7},{10,8},{11,9},{12,... | collective-permute-start | bytes 98312 | tf_op jit(solution)/shard_map/ppermute | solution.py:284
  7.3 9.9 %collective-permute-start.3 = (f32[64,512]{1,0:T(8,128)S(1)}, f32[64,512]{1,0:T(8,128)S(1)}, u32[]{:S(2)}, u32[]{:S(2)}) collective-permute-start(f32[64,512]{1,0:T(8,128)S(1)} %pad_maximum_fusion.near), channel_id=1, source_target_pairs={{4,0},{3,1},{6,2},{5,3},{8,4},{7,5},{10,6},{9,7},{12,8},{11,9},{14... | collective-permute-start | bytes 393224 | tf_op jit(solution)/shard_map/ppermute | solution.py:284
  10.5 6.7 %collective-permute-start.4 = (f32[64,128]{1,0:T(8,128)S(1)}, f32[64,128]{1,0:T(8,128)S(1)}, u32[]{:S(2)}, u32[]{:S(2)}) collective-permute-start(f32[64,128]{1,0:T(8,128)S(1)} %fusion), channel_id=1, source_target_pairs={{6,0},{5,1},{8,2},{7,3},{10,4},{9,5},{12,6},{11,7},{14,8},{13,9},{... | collective-permute-start | bytes 98312 | tf_op jit(solution)/shard_map/ppermute | solution.py:284
  24.2 6.4 %collective-permute-start.5 = (f32[4,128]{1,0:T(4,128)S(1)}, f32[4,128]{1,0:T(4,128)S(1)}, u32[]{:S(2)}, u32[]{:S(2)}) collective-permute-start(f32[4,128]{1,0:T(4,128)S(1)} %get-tuple-element.10), channel_id=1, source_target_pairs={{1,3},{0,4},{3,5},{2,6},{5,7},{4,8},{7,9},{6,10},{9,11},{8,12},{11... | collective-permute-start | bytes 6152 | tf_op jit(solution)/shard_map/ppermute | solution.py:284
  30.6 3.6 %collective-permute-start.6 = (f32[4,128]{1,0:T(4,128)S(1)}, f32[4,128]{1,0:T(4,128)S(1)}, u32[]{:S(2)}, u32[]{:S(2)}) collective-permute-start(f32[4,128]{1,0:T(4,128)S(1)} %select_minimum_fusion), channel_id=1, source_target_pairs={{0,1},{1,0},{2,3},{3,2},{4,5},{5,4},{6,7},{7,6},{8,9},{9,8},{10,11... | collective-permute-start | bytes 6152 | tf_op jit(solution)/shard_map/ppermute | solution.py:287
where the time goes:
time: 35.1 us; the launch traced here: 34.8 us
  Pallas kernels  11.6 us (33%)
  starting transfers between devices  11.5 us (33%)
  waiting for transfers between devices  9.28 us (26%)
  other arithmetic  1.47 us (4%)
  between operations  0.78 us (2%)
    ppermute x4, starting transfers between devices, shifted(): return lax.ppermute(value, axes, pairs)  9.12 us
    pallas_call x1, Pallas kernels, crossed(): pl.pallas_call(cross_body, out_shape=[sized(4, count // 4)] * 2 + [sized(...  7.01 us
    ppermute x2, waiting for transfers between devices, swapped(): lax.ppermute(value, 'chan', [(c, chans - 1 - c) for c in range(chans)])  4.86 us
    ppermute x4, waiting for transfers between devices, shifted(): return lax.ppermute(value, axes, pairs)  4.42 us
    pallas_call x1, Pallas kernels, prepare(): pl.pallas_call(own_body, out_shape=sized(count, channels * window, dtype=...  2.63 us
    pallas_call x1, Pallas kernels, paired(): pl.pallas_call(pair_body, out_shape=sized(4, count // 4), in_specs=[SMEM]...  1.92 us
    ppermute x2, starting transfers between devices, swapped(): lax.ppermute(value, 'chan', [(c, chans - 1 - c) for c in range(chans)])  1.72 us
    concatenate x1, other arithmetic, profile(): jnp.concatenate([series, tail, spare], axis=1)  0.87 us
  transfers between devices with their start and end apart: 7, of which 4 were waited for; matrix products, arithmetic and copies ran while one was open for 3% of the time, Pallas kernels for 13%

commit v1 on v0

--- a/solution.py
+++ b/solution.py
@@ -142,9 +142,6 @@
     product = contract(mine[:, pl.ds(block_of(0), WIDTH * LANES)], stage_a[...])
     pair_out[...] = product
     statistics(value, (sums_a, sums_b), (moments_a, moments_b), means, scales)
-    staged(mine, stage_b, block_of(1), info[1])
-    product = contract(mine[:, pl.ds(block_of(1), WIDTH * LANES)], stage_b[...])
-    pair_out[...] = pair_out[...] + product
     zeds = (zed_a, zed_b)
     cross[...] = jnp.zeros_like(cross)
     fill(samples, means, scales, zed_a, 0, 0)
@@ -179,11 +176,11 @@
         pl.multiple_of(2 * quarter + chan * quarter, quarter),
     ]
     blocks = mine.shape[1] // (WIDTH * LANES)
-    for slot in range(2):
-        base = block_of(blocks - 2 + slot)
-        staged(mine, stages[slot], base, chan)
-        value = contract(mine[:, pl.ds(base, WIDTH * LANES)], stages[slot][...])
-        pair[...] = (pair if slot else partial)[...] + value
+    for index, block in enumerate(range(1, blocks)):
+        stage = stages[index % 2]
+        staged(mine, stage, block_of(block), chan)
+        value = contract(mine[:, pl.ds(block_of(block), WIDTH * LANES)], stage[...])
+        pair[...] = (pair if index else partial)[...] + value
     near = []
     for index, start in enumerate(starts):
         value = pair[:, index * quarter : (index + 1) * quarter]

time: 35.1 us -> 34.3 us (0.977)
  the two profiles are of different devices: /device:TPU:24 before, /device:TPU:0 now
where the time goes in v1:
time: 34.3 us; the launch traced here: 34 us
  starting transfers between devices  12.2 us (36%)
  Pallas kernels  11.3 us (33%)
  waiting for transfers between devices  8.07 us (24%)
  other arithmetic  1.48 us (4%)
  between operations  0.81 us (2%)
    ppermute x4, starting transfers between devices, shifted(): return lax.ppermute(value, axes, pairs)  8.4 us
    pallas_call x1, Pallas kernels, crossed(): pl.pallas_call(cross_body, out_shape=[sized(4, count // 4)] * 2 + [sized(...  6.22 us
    ppermute x2, waiting for transfers between devices, swapped(): lax.ppermute(value, 'chan', [(c, chans - 1 - c) for c in range(chans)])  4.3 us
    ppermute x4, waiting for transfers between devices, shifted(): return lax.ppermute(value, axes, pairs)  3.77 us
    ppermute x2, starting transfers between devices, swapped(): lax.ppermute(value, 'chan', [(c, chans - 1 - c) for c in range(chans)])  3.13 us
    pallas_call x1, Pallas kernels, prepare(): pl.pallas_call(own_body, out_shape=sized(count, channels * window, dtype=...  2.63 us
    pallas_call x1, Pallas kernels, paired(): pl.pallas_call(pair_body, out_shape=sized(4, count // 4), in_specs=[SMEM]...  2.46 us
    concatenate x1, other arithmetic, profile(): jnp.concatenate([series, tail, spare], axis=1)  0.87 us
  transfers between devices with their start and end apart: 7, of which 3 were waited for; matrix products, arithmetic and copies ran while one was open for 3% of the time, Pallas kernels for 15%

profile of v1, /device:TPU:0, one launch (start us, length us, event | category | flops | bytes accessed | tf_op | source)
XLA Modules:
  0.0 34.0 jit_solution(6630212456179223424)
XLA Ops:
  0.0 0.7 %collective-permute-start.2 = (f32[32,127]{1,0:T(8,128)}, f32[32,127]{1,0:T(8,128)S(1)}, u32[]{:S(2)}, u32[]{:S(2)}) collective-permute-start(f32[32,127]{1,0:T(8,128)} %param.4), channel_id=1, source_target_pairs={{26,27},{27,26},{28,29},{29,28},{30,31},{31,30}} | collective-permute-start | bytes 48776 | tf_op jit(solution)/shard_map/ppermute | solution.py:293
  0.7 3.1 %collective-permute-start = (f32[32,512]{1,0:T(8,128)}, f32[32,512]{1,0:T(8,128)S(1)}, u32[]{:S(2)}, u32[]{:S(2)}) collective-permute-start(f32[32,512]{1,0:T(8,128)} %param.3), channel_id=1, source_target_pairs={{0,1},{1,0},{2,3},{3,2},{4,5},{5,4},{6,7},{7,6},{8,9},{9,8},{10,11... | collective-permute-start | bytes 196616 | tf_op jit(solution)/shard_map/ppermute | solution.py:284
  3.7 0.1 pad.7.clone
  3.8 0.9 %maximum_maximum_fusion = f32[32,640]{1,0:T(8,128)S(1)} fusion(f32[32,127]{1,0:T(8,128)} %param.4, f32[32,512]{1,0:T(8,128)} %param.3, f32[640]{0:T(1024)S(1)} %pad.7.clone), kind=kLoop, calls=%fused_computation.3 | loop fusion | flops 40960 | bytes 166272 | tf_op jit(solution)/shard_map/concatenate | solution.py:294
  5.4 0.1 stack.35.info
  5.4 0.7 %collective-permute-done = f32[32,512]{1,0:T(8,128)S(1)} collective-permute-done((f32[32,512]{1,0:T(8,128)}, f32[32,512]{1,0:T(8,128)S(1)}, u32[]{:S(2)}, u32[]{:S(2)}) %collective-permute-start) | collective-permute-done | bytes 65568 | tf_op jit(solution)/shard_map/ppermute | solution.py:284
  6.2 1.3 %collective-permute-start.1 = (f32[64,128]{1,0:T(8,128)S(1)}, f32[64,128]{1,0:T(8,128)S(1)}, u32[]{:S(2)}, u32[]{:S(2)}) collective-permute-start(f32[64,128]{1,0:T(8,128)S(1)} %fusion), channel_id=1, source_target_pairs={{2,0},{3,1},{4,2},{5,3},{6,4},{7,5},{8,6},{9,7},{10,8},{11,9},{12,... | collective-permute-start | bytes 98312 | tf_op jit(solution)/shard_map/ppermute | solution.py:281
  7.5 1.3 %collective-permute-start.3 = (f32[64,512]{1,0:T(8,128)S(1)}, f32[64,512]{1,0:T(8,128)S(1)}, u32[]{:S(2)}, u32[]{:S(2)}) collective-permute-start(f32[64,512]{1,0:T(8,128)S(1)} %pad_maximum_fusion.near), channel_id=1, source_target_pairs={{4,0},{3,1},{6,2},{5,3},{8,4},{7,5},{10,6},{9,7},{12,8},{11,9},{14... | collective-permute-start | bytes 393224 | tf_op jit(solution)/shard_map/ppermute | solution.py:281
  8.8 0.0 collective-permute-done.2
  8.8 1.3 %collective-permute-start.4 = (f32[64,128]{1,0:T(8,128)S(1)}, f32[64,128]{1,0:T(8,128)S(1)}, u32[]{:S(2)}, u32[]{:S(2)}) collective-permute-start(f32[64,128]{1,0:T(8,128)S(1)} %fusion), channel_id=1, source_target_pairs={{6,0},{5,1},{8,2},{7,3},{10,4},{9,5},{12,6},{11,7},{14,8},{13,9},{... | collective-permute-start | bytes 98312 | tf_op jit(solution)/shard_map/ppermute | solution.py:281
  10.1 0.0 collective-permute-done.1.head
  10.1 2.6 %shard_map.37.mine = bf16[512,8192]{1,0:T(8,128)(2,1)S(1)} custom-call(s32[6]{0:T(128)S(1)} %stack.35.info, f32[64,512]{1,0:T(8,128)S(1)} %pad_maximum_fusion.near, f32[64,128]{1,0:T(8,128)S(1)} %collective-permute-done.1.head, f32[64,128]{1,0:T(8,128)S(1)} %select_maximum_fusion.tail), custom_call_target="tpu_custom_call" | custom-call | flops 419430400 | bytes 2097152 | tf_op jit(solution)/shard_map/pallas_call | solution.py:220
  12.8 3.8 %collective-permute-done.4.head = f32[64,128]{1,0:T(8,128)S(1)} collective-permute-done((f32[64,128]{1,0:T(8,128)S(1)}, f32[64,128]{1,0:T(8,128)S(1)}, u32[]{:S(2)}, u32[]{:S(2)}) %collective-permute-start.4) | collective-permute-done | bytes 32800 | tf_op jit(solution)/shard_map/ppermute | solution.py:281
  16.5 0.0 collective-permute-done.3.other
  16.5 6.2 %shard_map.38 = (f32[4,128]{1,0:T(4,128)S(1)}, f32[4,128]{1,0:T(4,128)S(1)}, f32[512,256]{1,0:T(8,128)S(1)}) custom-call(s32[6]{0:T(128)S(1)} %stack.35.info, bf16[512,8192]{1,0:T(8,128)(2,1)S(1)} %shard_map.37.mine, f32[64,512]{1,0:T(8,128)S(1)} %collective-permute-done.3.other, f32[64,128]{1,0:T(8,128)S(1)} %collective-permute-done.4.head, ...), custom_call_target="tpu_custom_call" | custom-call | flops 4294967296 | bytes 2097152 | tf_op jit(solution)/shard_map/pallas_call | solution.py:233
  22.7 4.5 %collective-permute-start.5 = (f32[4,128]{1,0:T(4,128)S(1)}, f32[4,128]{1,0:T(4,128)S(1)}, u32[]{:S(2)}, u32[]{:S(2)}) collective-permute-start(f32[4,128]{1,0:T(4,128)S(1)} %get-tuple-element.10), channel_id=1, source_target_pairs={{1,3},{0,4},{3,5},{2,6},{5,7},{4,8},{7,9},{6,10},{9,11},{8,12},{11... | collective-permute-start | bytes 6152 | tf_op jit(solution)/shard_map/ppermute | solution.py:281
  27.3 2.5 %shard_map.39 = f32[4,128]{1,0:T(4,128)S(1)} custom-call(s32[6]{0:T(128)S(1)} %stack.35.info, bf16[512,8192]{1,0:T(8,128)(2,1)S(1)} %shard_map.37.mine, f32[4,128]{1,0:T(4,128)S(1)} %get-tuple-element.8.part, f32[512,256]{1,0:T(8,128)S(1)} %get-tuple-element.9.partial), custom_call_target="tpu_custom_call" | custom-call | flops 2147483648 | bytes 2097152 | tf_op jit(solution)/shard_map/pallas_call | solution.py:250
  29.8 0.0 collective-permute-done.5
  29.8 0.1 collective-permute-start.6
  29.9 3.6 %collective-permute-done.6 = f32[4,128]{1,0:T(4,128)S(1)} collective-permute-done((f32[4,128]{1,0:T(4,128)S(1)}, f32[4,128]{1,0:T(4,128)S(1)}, u32[]{:S(2)}, u32[]{:S(2)}) %collective-permute-start.6) | collective-permute-done | bytes 2080 | tf_op jit(solution)/shard_map/ppermute | solution.py:284
  33.4 0.6 %minimum_bitcast_fusion = f32[512]{0:T(512)} fusion(f32[4,128]{1,0:T(4,128)S(1)} %select_minimum_fusion, f32[4,128]{1,0:T(4,128)S(1)} %collective-permute-done.6), kind=kLoop, calls=%fused_computation.7 | loop fusion | flops 512 | bytes 6144 | tf_op jit(solution)/shard_map/reshape | solution.py:306
  (6 shorter events, 0.0 us)
Async XLA Ops:
  0.0 8.8 %collective-permute-start.2 = (f32[32,127]{1,0:T(8,128)}, f32[32,127]{1,0:T(8,128)S(1)}, u32[]{:S(2)}, u32[]{:S(2)}) collective-permute-start(f32[32,127]{1,0:T(8,128)} %param.4), channel_id=1, source_target_pairs={{26,27},{27,26},{28,29},{29,28},{30,31},{31,30}} | collective-permute-start | bytes 48776 | tf_op jit(solution)/shard_map/ppermute | solution.py:293
  0.7 5.5 %collective-permute-start = (f32[32,512]{1,0:T(8,128)}, f32[32,512]{1,0:T(8,128)S(1)}, u32[]{:S(2)}, u32[]{:S(2)}) collective-permute-start(f32[32,512]{1,0:T(8,128)} %param.3), channel_id=1, source_target_pairs={{0,1},{1,0},{2,3},{3,2},{4,5},{5,4},{6,7},{7,6},{8,9},{9,8},{10,11... | collective-permute-start | bytes 196616 | tf_op jit(solution)/shard_map/ppermute | solution.py:284
  6.2 3.9 %collective-permute-start.1 = (f32[64,128]{1,0:T(8,128)S(1)}, f32[64,128]{1,0:T(8,128)S(1)}, u32[]{:S(2)}, u32[]{:S(2)}) collective-permute-start(f32[64,128]{1,0:T(8,128)S(1)} %fusion), channel_id=1, source_target_pairs={{2,0},{3,1},{4,2},{5,3},{6,4},{7,5},{8,6},{9,7},{10,8},{11,9},{12,... | collective-permute-start | bytes 98312 | tf_op jit(solution)/shard_map/ppermute | solution.py:281
  7.5 9.0 %collective-permute-start.3 = (f32[64,512]{1,0:T(8,128)S(1)}, f32[64,512]{1,0:T(8,128)S(1)}, u32[]{:S(2)}, u32[]{:S(2)}) collective-permute-start(f32[64,512]{1,0:T(8,128)S(1)} %pad_maximum_fusion.near), channel_id=1, source_target_pairs={{4,0},{3,1},{6,2},{5,3},{8,4},{7,5},{10,6},{9,7},{12,8},{11,9},{14... | collective-permute-start | bytes 393224 | tf_op jit(solution)/shard_map/ppermute | solution.py:281
  8.8 7.7 %collective-permute-start.4 = (f32[64,128]{1,0:T(8,128)S(1)}, f32[64,128]{1,0:T(8,128)S(1)}, u32[]{:S(2)}, u32[]{:S(2)}) collective-permute-start(f32[64,128]{1,0:T(8,128)S(1)} %fusion), channel_id=1, source_target_pairs={{6,0},{5,1},{8,2},{7,3},{10,4},{9,5},{12,6},{11,7},{14,8},{13,9},{... | collective-permute-start | bytes 98312 | tf_op jit(solution)/shard_map/ppermute | solution.py:281
  22.7 7.0 %collective-permute-start.5 = (f32[4,128]{1,0:T(4,128)S(1)}, f32[4,128]{1,0:T(4,128)S(1)}, u32[]{:S(2)}, u32[]{:S(2)}) collective-permute-start(f32[4,128]{1,0:T(4,128)S(1)} %get-tuple-element.10), channel_id=1, source_target_pairs={{1,3},{0,4},{3,5},{2,6},{5,7},{4,8},{7,9},{6,10},{9,11},{8,12},{11... | collective-permute-start | bytes 6152 | tf_op jit(solution)/shard_map/ppermute | solution.py:281
  29.8 3.7 %collective-permute-start.6 = (f32[4,128]{1,0:T(4,128)S(1)}, f32[4,128]{1,0:T(4,128)S(1)}, u32[]{:S(2)}, u32[]{:S(2)}) collective-permute-start(f32[4,128]{1,0:T(4,128)S(1)} %select_minimum_fusion), channel_id=1, source_target_pairs={{0,1},{1,0},{2,3},{3,2},{4,5},{5,4},{6,7},{7,6},{8,9},{9,8},{10,11... | collective-permute-start | bytes 6152 | tf_op jit(solution)/shard_map/ppermute | solution.py:284
